TPU v7x, 32 devices: a whole 2x2x4 slice. The times are simulated.
32 devices in a mesh: tok: 4 (over y, core), tp: 8 (over z, x).
Axes of the slice: x: 2, y: 2, z: 4, core: 2. Of those that a mesh axis runs over, the one named last changes fastest.
Arguments:
- residual: bfloat16 [1024, 16384], P('tok', 'tp')
- norm_gain: float32 [16384], replicated, may hold values from 0.5 to 1.5
- weight: bfloat16 [30720, 16384], P(('tok', 'tp')), may hold values from -6 to 6
- scale_codes: int32 [30720, 2], P(('tok', 'tp')), may hold values from 0 to 7
- zero_points: int32 [30720, 2], P(('tok', 'tp')), may hold values from 4 to 11
- panels: bfloat16 [256, 16384], P(None, ('tok', 'tp')), as said below
Outputs:
- gram: float32 [16384, 16384], P('tok', 'tp')
- quantized: bfloat16 [30720, 16384], P('tok', 'tp')
Inputs may be any that keep to these rules, and one draw needn't show every extreme that they name: Row j of panels is row j of an upper-triangular factor: entries left of column j are zero and panels[j, j] lies in [0.5, 1.5].
All inputs are finite; a program needn't handle non-finite values.
Results may differ from a plain program's by a relative error of at most 0.0085.
Values may be sent and summed in bfloat16 or wider, within the bound.
A program may use at most 384 MiB of HBM per device.

v0:
```python
import math
import jax
import jax.numpy as jnp
from jax import lax
from jax.sharding import PartitionSpec as P

BLOCK = 128
BLOCKS = 2
EPS = 1e-05
SOFTNESS = 0.9
FULL_TURN = 2.0 * math.pi
HIGHEST = lax.Precision.HIGHEST


def spread(x, axis, root):
    mine = lax.axis_index(axis) == root
    return lax.psum(jnp.where(mine, x, jnp.zeros_like(x)), axis)


def dequantize(column, scale_row, zero_row):
    shifted = column / scale_row + zero_row
    softened = shifted - SOFTNESS * jnp.sin(FULL_TURN * shifted) / FULL_TURN
    return scale_row * (jnp.clip(softened, 0.0, 15.0) - zero_row)


def block_errors(block_cols, diagonal, scale_row, zero_row):
    row_count = block_cols.shape[0]
    block_width = block_cols.shape[1]
    lane_ids = lax.iota(jnp.int32, 8)
    wide_ids = lax.iota(jnp.int32, block_width)

    def sub_step(step_index, carried):
        block_now, errors = carried
        sub_first = step_index * 8
        sub_cols = lax.dynamic_slice_in_dim(block_now, sub_first, 8, 1)
        sub_panel = lax.dynamic_slice_in_dim(diagonal, sub_first, 8, 0)
        local_pivots = lax.dynamic_slice_in_dim(sub_panel, sub_first, 8, 1)
        collected = []
        for i in range(8):
            column_now = sub_cols[:, i]
            restored = dequantize(column_now, scale_row, zero_row)
            error_now = (column_now - restored) / local_pivots[i, i]
            sub_cols = (
                sub_cols
                - error_now[:, None] * jnp.where(lane_ids > i, local_pivots[i], 0.0)[None, :]
            )
            sub_cols = jnp.where((lane_ids == i)[None, :], restored[:, None], sub_cols)
            collected.append(error_now)
        sub_errors = jnp.stack(collected, axis=1)
        spill_over = jnp.dot(sub_errors, sub_panel, precision=HIGHEST)
        block_now = jnp.where(
            (wide_ids >= sub_first + 8)[None, :], block_now - spill_over, block_now
        )
        block_now = lax.dynamic_update_slice_in_dim(block_now, sub_cols, sub_first, 1)
        errors = lax.dynamic_update_slice_in_dim(errors, sub_errors, sub_first, 1)
        return (block_now, errors)

    start_state = (block_cols, jnp.zeros((row_count, block_width), jnp.float32))
    return lax.fori_loop(0, block_width // 8, sub_step, start_state)


def on_device(residual, norm_gain, weight, scale_codes, zero_points, panels):
    tok_local, feat_local = residual.shape
    tp_count = lax.axis_size("tp")
    tok_count = lax.axis_size("tok")
    feat_total = feat_local * tp_count
    tp_place = lax.axis_index("tp")
    local_rows = residual.astype(jnp.float32)
    row_sums = lax.psum(jnp.sum(local_rows * local_rows, axis=1), "tp")
    gain_own = lax.dynamic_slice_in_dim(norm_gain, tp_place * feat_local, feat_local, 0)
    x_own = (
        local_rows * lax.rsqrt(row_sums[:, None] / feat_total + EPS) * gain_own[None, :]
    ).astype(jnp.bfloat16)
    x_full = lax.all_gather(x_own, "tp", axis=1, tiled=True)
    gram_sum = lax.psum_scatter(
        lax.dot_general(
            x_full, x_own, (((0,), (0,)), ((), ())), preferred_element_type=jnp.float32
        ).astype(jnp.bfloat16),
        "tok",
        scatter_dimension=0,
        tiled=True,
    ).astype(jnp.float32)
    gram = gram_sum / (tok_local * tok_count)
    shard_cols = panels.shape[1]
    working = weight.astype(jnp.float32)
    column = lax.iota(jnp.int32, feat_total)
    for k in range(BLOCKS):
        block_start = k * BLOCK
        scale_row = jnp.exp2(scale_codes[:, k].astype(jnp.float32) * 0.5 - 3.0)
        zero_row = zero_points[:, k].astype(jnp.float32)
        root_index = block_start // shard_cols
        offset_cols = block_start - root_index * shard_cols
        own_block = panels[block_start : block_start + BLOCK, offset_cols : offset_cols + BLOCK]
        diagonal = spread(own_block, ("tok", "tp"), root_index).astype(jnp.float32)
        block_cols, errors = block_errors(
            working[:, block_start : block_start + BLOCK], diagonal, scale_row, zero_row
        )
        correction = jnp.dot(
            errors,
            lax.all_gather(
                panels[block_start : block_start + BLOCK], ("tok", "tp"), axis=1, tiled=True
            ).astype(jnp.float32),
            precision=HIGHEST,
        )
        working = jnp.where((column >= block_start + BLOCK)[None, :], working - correction, working)
        working = lax.dynamic_update_slice_in_dim(working, block_cols, block_start, 1)
    quantized = lax.all_to_all(
        working.astype(jnp.bfloat16), "tp", split_axis=1, concat_axis=0, tiled=True
    )
    return (gram, quantized)


def solution(mesh):
    in_specs = (
        P("tok", "tp"),
        P(),
        P(("tok", "tp"), None),
        P(("tok", "tp"), None),
        P(("tok", "tp"), None),
        P(None, ("tok", "tp")),
    )
    out_specs = (P("tok", "tp"), P("tok", "tp"))
    return jax.shard_map(
        on_device, mesh=mesh, in_specs=in_specs, out_specs=out_specs, check_vma=False
    )
```

profile of v0, /device:TPU:1, one launch (start us, length us, event | category | flops | bytes accessed | tf_op | source)
XLA Modules:
  0.0 1459.3 jit_solution(8556736024828552044)
XLA Ops:
  7.2 1.4 slice_select_fusion
  8.7 1.7 fusion.67
  11.2 1.5 fusion.62
  12.7 18.7 %psum.21 = f32[256]{0:T(256)S(1)} all-reduce(f32[256]{0:T(256)S(1)} %fusion.62), channel_id=1, replica_groups=mesh['tok'=4,'tp'=8] {'tp'}, use_global_device_ids=true, to_apply=%region_1.0 | all-reduce | flops 256 | bytes 2048 | tf_op jit(solution)/shard_map/psum | solution.py:69
  31.4 2.5 fusion.64
  37.4 100.4 %all-reduce.4.cloned.1.call-done = (bf16[128,128]{1,0:T(8,128)(2,1)}, bf16[128,128]{1,0:T(8,128)(2,1)}) async-done(((bf16[128,128]{1,0:T(8,128)(2,1)}, bf16[128,128]{1,0:T(8,128)(2,1)}), (bf16[128,128]{1,0:T(8,128)(2,1)}, bf16[128,128]{1,0:T(8,128)(2,1)})) %all-reduce.4.cloned.1.call-update) | async-done | bytes 65552 | tf_op jit(solution)/shard_map/psum | solution.py:17
  138.6 221.0 %while.40 = (s32[]{:T(128)}, f32[960,128]{0,1:T(8,128)S(1)}, f32[960,128]{0,1:T(8,128)S(1)}, f32[960]{0:T(1024)S(1)}, f32[960]{0:T(1024)S(1)}, /*index=5*/f32[12...) while((s32[]{:T(128)}, f32[960,128]{0,1:T(8,128)S(1)}, ...), condition=%wide.region_5.6_spmd.clone.clone, body=%wide.region_4.5_spmd.clone.clone.sunk | while | flops 12948808 | bytes 4160943 | solution.py:59
  147.7 3.7 dynamic_update_slice.69
  160.8 4.5 dynamic_update_slice.69
  174.6 4.5 dynamic_update_slice.69
  188.5 4.5 dynamic_update_slice.69
  202.4 4.5 dynamic_update_slice.69
  216.2 4.5 dynamic_update_slice.69
  230.1 4.5 dynamic_update_slice.69
  244.0 4.5 dynamic_update_slice.69
  257.8 4.5 dynamic_update_slice.69
  271.7 4.5 dynamic_update_slice.69
  285.5 4.5 dynamic_update_slice.69
  299.4 4.5 dynamic_update_slice.69
  313.3 4.5 dynamic_update_slice.69
  327.1 4.5 dynamic_update_slice.69
  341.0 4.5 dynamic_update_slice.69
  354.8 4.5 dynamic_update_slice.69
  360.5 42.3 %subtract_select_fusion.17 = f32[960,16384]{1,0:T(8,128)} fusion(f32[960,128]{0,1:T(8,128)S(1)} %get-tuple-element.574, bf16[128,16384]{1,0:T(8,128)(2,1)} %all-gather.6.cloned.1.call-done, pred[16384]{0:T(1024)(128)(4,1)S(1)} %iota_compare_fusion.34, bf16[960,16384]{1,0:T(8,128)(2,1)} %param.12), kind=kOutput, calls=%fused_computation.145 | convolution fusion | flops 24206376960 | bytes 99074048 | tf_op jit(solution)/shard_map/dot_general | solution.py:98
  403.7 1.1 slice.679
  405.0 29.4 %convolution_convert_fusion = bf16[16384,2048]{1,0:T(8,128)(2,1)} fusion(bf16[256,16384]{1,0:T(8,128)(2,1)} %all-gather.4.cloned.1.call-done, bf16[256,2048]{1,0:T(8,128)(2,1)S(1)} %copy-done), kind=kOutput, calls=%fused_computation.146 | convolution fusion | flops 17213423616 | bytes 76546048 | tf_op jit(solution)/shard_map/dot_general | solution.py:76
  434.5 226.1 %while.41 = (s32[]{:T(128)}, f32[960,128]{0,1:T(8,128)S(1)}, f32[960,128]{0,1:T(8,128)S(1)}, f32[960]{0:T(1024)S(1)}, f32[960]{0:T(1024)S(1)}, /*index=5*/f32[12...) while((s32[]{:T(128)}, f32[960,128]{0,1:T(8,128)S(1)}, ...), condition=%wide.region_8.9_spmd.clone.clone, body=%wide.region_7.8_spmd.clone.clone.sunk | while | flops 12948808 | bytes 4160943 | solution.py:59
  444.1 3.7 dynamic_update_slice.71
  457.5 4.5 dynamic_update_slice.71
  471.7 4.5 dynamic_update_slice.71
  485.9 4.5 dynamic_update_slice.71
  500.1 4.5 dynamic_update_slice.71
  514.2 4.5 dynamic_update_slice.71
  528.4 4.5 dynamic_update_slice.71
  542.6 4.5 dynamic_update_slice.71
  556.7 4.5 dynamic_update_slice.71
  570.9 4.5 dynamic_update_slice.71
  585.1 4.5 dynamic_update_slice.71
  599.2 4.5 dynamic_update_slice.71
  613.4 4.5 dynamic_update_slice.71
  627.6 4.5 dynamic_update_slice.71
  641.7 4.5 dynamic_update_slice.71
  655.9 4.5 dynamic_update_slice.71
  660.8 41.6 %subtract_select_fusion.16 = bf16[960,16384]{1,0:T(8,128)(2,1)} fusion(f32[960,16384]{1,0:T(8,128)} %constant_dynamic-update-slice_fusion.3, f32[960,128]{0,1:T(8,128)S(1)} %get-tuple-element.576, bf16[128,16384]{1,0:T(8,128)(2,1)} %all-gather.8.cloned.1.call-done, pred[16384]{0:T(1024)(128)(4,1)S(1)} %iota_compare_fusion.35), kind=kOutput, calls=%fused_computation.144 | convolution fusion | flops 24190648320 | bytes 99074048 | tf_op jit(solution)/shard_map/dot_general | solution.py:98
  703.2 21.7 %copy.170 = bf16[120,8,8,2048]{3,2,0,1:T(8,128)(2,1)} copy(bf16[120,8,8,2048]{3,2,1,0:T(8,128)(2,1)} %bitcast.316) | data formatting | bytes 62914560 | tf_op jit(solution)/shard_map/all_to_all | solution.py:107
  724.9 687.8 %all_to_all.19 = bf16[960,8,2048]{2,0,1:T(8,128)(2,1)} all-to-all(bf16[960,8,2048]{2,0,1:T(8,128)(2,1)} %bitcast.318), channel_id=1, replica_groups=mesh['tok'=4,'tp'=8] {'tp'}, dimensions={1} | all-to-all | bytes 62914560 | tf_op jit(solution)/shard_map/all_to_all | solution.py:107
  1412.6 18.8 %convert_multiply_fusion = f32[4096,2048]{1,0:T(8,128)} fusion(bf16[4096,2048]{1,0:T(8,128)(2,1)} %reduce-scatter.4.cloned.1.call-done), kind=kLoop, calls=%fused_computation.147 | loop fusion | flops 16777216 | bytes 50331648 | tf_op jit(solution)/shard_map/div | solution.py:83
  1431.4 21.3 %copy.210 = bf16[7680,2048]{1,0:T(8,128)(2,1)} copy(bf16[7680,2048]{1,0:T(8,128)(2,1)} %bitcast.317) | data formatting | bytes 62914560
  (1121 shorter events, 308.1 us)
Async XLA Ops:
  7.2 130.6 %all-reduce.4.cloned.1.call-start = ((), (), s32[]{:S(2)}) async-start(), calls=%async_computation.6 | async-start | bytes 131072 | tf_op jit(solution)/shard_map/psum | solution.py:17
  8.7 351.9 %all-gather.6.cloned.1.call-start = ((), (), s32[]{:S(2)}) async-start(), calls=%async_computation.3 | async-start | bytes 4325376 | tf_op jit(solution)/shard_map/all_gather | solution.py:100
  10.4 394.6 %all-gather.4.cloned.1.call-start = ((), (), s32[]{:S(2)}) async-start(), calls=%async_computation.2 | async-start | bytes 9437184 | tf_op jit(solution)/shard_map/all_gather | solution.py:74
  33.9 626.9 %all-gather.8.cloned.1.call-start = ((), (), s32[]{:S(2)}) async-start(), calls=%async_computation.4 | async-start | bytes 4325376 | tf_op jit(solution)/shard_map/all_gather | solution.py:100
  34.5 1378.1 %reduce-scatter.4.cloned.1.call-start = ((), (), s32[]{:S(2)}) async-start(), calls=%async_computation.5 | async-start | bytes 83886080
  360.5 44.5 %copy-start = (bf16[256,2048]{1,0:T(8,128)(2,1)S(1)}, bf16[256,2048]{1,0:T(8,128)(2,1)}, u32[]{:S(2)}) copy-start(bf16[256,2048]{1,0:T(8,128)(2,1)} %fusion.64) | copy-start | bytes 3145732
Sparse Core Ops, SparseCore 0:
  13.7 124.0 all-reduce.3
  140.6 62.9 all-gather.5
  206.4 121.5 all-gather.3
  331.3 62.2 all-gather.7
  434.5 445.9 reduce-scatter.3
where the time goes:
time: 1460 us
  blocking collectives  706 us (48%)
  other arithmetic  251 us (17%)
  local copies, waits for them, and re-layouts  237 us (16%)
  matrix products  144 us (10%)
  waiting for transfers between devices  101 us (7%)
    all_to_all x1, blocking collectives, on_device(): lax.all_to_all(working.astype(jnp.bfloat16), 'tp', split_axis=1, concat_a...  688 us
    div x256, other arithmetic, sub_step(): error_now = (column_now - restored) / local_pivots[i, i]  197 us
    dynamic_update_slice x32, local copies, waits for them, and re-layouts, sub_step(): lax.dynamic_update_slice_in_dim(block_now, sub_cols, sub_first, 1)  142 us
    psum x1, waiting for transfers between devices, spread(): return lax.psum(jnp.where(mine, x, jnp.zeros_like(x)), axis)  100 us
    dot_general x2, matrix products, on_device(): jnp.dot(errors, lax.all_gather(panels[block_start:block_start + BLOCK], (...  84 us
    dot_general x32, matrix products, sub_step(): spill_over = jnp.dot(sub_errors, sub_panel, precision=HIGHEST)  30.6 us
    dot_general x1, matrix products, on_device(): lax.dot_general(x_full, x_own, (((0,), (0,)), ((), ())), preferred_elemen...  29.4 us
  transfers between devices with their start and end apart: 5, of which 1 were waited for; matrix products, arithmetic and copies ran while one was open for 40% of the time, Pallas kernels for 0%

commit v1 on v0

--- a/solution.py
+++ b/solution.py
@@ -14,7 +14,7 @@
 
 def spread(x, axis, root):
     mine = lax.axis_index(axis) == root
-    return lax.psum(jnp.where(mine, x, jnp.zeros_like(x)), axis)
+    return jnp.sum(lax.all_gather(jnp.where(mine, x, jnp.zeros_like(x)), axis), axis=0)
 
 
 def dequantize(column, scale_row, zero_row):

time: 1460 us -> 1400 us (0.959)
  waiting for transfers between devices: 101 us -> 30.5 us
    psum x1 -> x0, waiting for transfers between devices: 100 us -> none  [spread(): return lax.psum(jnp.where(mine, x, jnp.zeros_like(x)), axis)]
    all_gather x0 -> x2, waiting for transfers between devices: none -> 29.1 us  [spread(): lax.all_gather(jnp.where(mine, x, jnp.zeros_like(x)), axis)]
  transfers between devices with their start and end apart: 5 -> 6, of which waited for: 1 -> 1; matrix products, arithmetic and copies ran while one was open for 40% -> 43% of each run, Pallas kernels for 0% -> 0%
where the time goes in v1:
time: 1400 us; the launch traced here: 1390 us
  blocking collectives  707 us (50%)
  other arithmetic  256 us (18%)
  local copies, waits for them, and re-layouts  237 us (17%)
  matrix products  144 us (10%)
  waiting for transfers between devices  30.5 us (2%)
  between operations  14.3 us (1%)
    all_to_all x1, blocking collectives, on_device(): lax.all_to_all(working.astype(jnp.bfloat16), 'tp', split_axis=1, concat_a...  688 us
    div x256, other arithmetic, sub_step(): error_now = (column_now - restored) / local_pivots[i, i]  201 us
    dynamic_update_slice x32, local copies, waits for them, and re-layouts, sub_step(): lax.dynamic_update_slice_in_dim(block_now, sub_cols, sub_first, 1)  142 us
    dot_general x2, matrix products, on_device(): jnp.dot(errors, lax.all_gather(panels[block_start:block_start + BLOCK], (...  83.7 us
    dot_general x32, matrix products, sub_step(): spill_over = jnp.dot(sub_errors, sub_panel, precision=HIGHEST)  30.6 us
    dot_general x1, matrix products, on_device(): lax.dot_general(x_full, x_own, (((0,), (0,)), ((), ())), preferred_elemen...  29.4 us
    all_gather x2, waiting for transfers between devices, spread(): lax.all_gather(jnp.where(mine, x, jnp.zeros_like(x)), axis)  29.1 us
  transfers between devices with their start and end apart: 6, of which 1 were waited for; matrix products, arithmetic and copies ran while one was open for 43% of the time, Pallas kernels for 0%

profile of v1, /device:TPU:1, one launch (start us, length us, event | category | flops | bytes accessed | tf_op | source)
XLA Modules:
  0.0 1393.6 jit_solution(5015774351228854354)
XLA Ops:
  7.2 1.4 slice_select_fusion
  9.5 1.7 fusion.67
  11.9 1.5 fusion.62
  13.4 18.7 %psum.7 = f32[256]{0:T(256)S(1)} all-reduce(f32[256]{0:T(256)S(1)} %fusion.62), channel_id=1, replica_groups=mesh['tok'=4,'tp'=8] {'tp'}, use_global_device_ids=true, to_apply=%region_1.0 | all-reduce | flops 256 | bytes 2048 | tf_op jit(solution)/shard_map/psum | solution.py:69
  32.2 2.5 fusion.64
  38.1 29.1 %all-gather.14.cloned.1.call-done = bf16[4096,128]{1,0:T(8,128)(2,1)} async-done(((bf16[128,128]{1,0:T(8,128)(2,1)}), bf16[4096,128]{1,0:T(8,128)(2,1)}) %all-gather.14.cloned.1.call-update) | async-done | bytes 1048592 | tf_op jit(solution)/shard_map/all_gather | solution.py:17
  68.7 225.4 %while.40 = (s32[]{:T(128)}, f32[960,128]{0,1:T(8,128)S(1)}, f32[960,128]{0,1:T(8,128)S(1)}, f32[960]{0:T(1024)S(1)}, f32[960]{0:T(1024)S(1)}, /*index=5*/f32[12...) while((s32[]{:T(128)}, f32[960,128]{0,1:T(8,128)S(1)}, ...), condition=%wide.region_5.6_spmd.clone.clone, body=%wide.region_4.5_spmd.clone.clone.sunk | while | flops 12948808 | bytes 4160943 | solution.py:59
  78.1 3.7 dynamic_update_slice.69
  91.5 4.5 dynamic_update_slice.69
  105.6 4.5 dynamic_update_slice.69
  119.7 4.5 dynamic_update_slice.69
  133.9 4.5 dynamic_update_slice.69
  148.0 4.5 dynamic_update_slice.69
  162.2 4.5 dynamic_update_slice.69
  176.3 4.5 dynamic_update_slice.69
  190.4 4.5 dynamic_update_slice.69
  204.6 4.5 dynamic_update_slice.69
  218.7 4.5 dynamic_update_slice.69
  232.8 4.5 dynamic_update_slice.69
  247.0 4.5 dynamic_update_slice.69
  261.1 4.5 dynamic_update_slice.69
  275.2 4.5 dynamic_update_slice.69
  289.4 4.5 dynamic_update_slice.69
  294.3 1.4 reduce_sum.35
  295.8 42.2 %subtract_select_fusion.17 = f32[960,16384]{1,0:T(8,128)} fusion(f32[960,128]{0,1:T(8,128)S(1)} %get-tuple-element.574, bf16[128,16384]{1,0:T(8,128)(2,1)} %all-gather.10.cloned.1.call-done, pred[16384]{0:T(1024)(128)(4,1)S(1)} %iota_compare_fusion.34, bf16[960,16384]{1,0:T(8,128)(2,1)} %param.12), kind=kOutput, calls=%fused_computation.145 | convolution fusion | flops 24206376960 | bytes 99074048 | tf_op jit(solution)/shard_map/dot_general | solution.py:98
  340.1 29.4 %convolution_convert_fusion = bf16[16384,2048]{1,0:T(8,128)(2,1)} fusion(bf16[256,16384]{1,0:T(8,128)(2,1)} %all-gather.8.cloned.1.call-done, bf16[256,2048]{1,0:T(8,128)(2,1)S(1)} %copy-done), kind=kOutput, calls=%fused_computation.146 | convolution fusion | flops 17213423616 | bytes 76546048 | tf_op jit(solution)/shard_map/dot_general | solution.py:76
  369.6 224.9 %while.41 = (s32[]{:T(128)}, f32[960,128]{0,1:T(8,128)S(1)}, f32[960,128]{0,1:T(8,128)S(1)}, f32[960]{0:T(1024)S(1)}, f32[960]{0:T(1024)S(1)}, /*index=5*/f32[12...) while((s32[]{:T(128)}, f32[960,128]{0,1:T(8,128)S(1)}, ...), condition=%wide.region_8.9_spmd.clone.clone, body=%wide.region_7.8_spmd.clone.clone.sunk | while | flops 12948808 | bytes 4160943 | solution.py:59
  379.2 3.7 dynamic_update_slice.71
  392.5 4.5 dynamic_update_slice.71
  406.6 4.5 dynamic_update_slice.71
  420.7 4.5 dynamic_update_slice.71
  434.9 4.5 dynamic_update_slice.71
  449.0 4.5 dynamic_update_slice.71
  463.1 4.5 dynamic_update_slice.71
  477.1 4.5 dynamic_update_slice.71
  491.2 4.5 dynamic_update_slice.71
  505.3 4.5 dynamic_update_slice.71
  519.4 4.5 dynamic_update_slice.71
  533.5 4.5 dynamic_update_slice.71
  547.5 4.5 dynamic_update_slice.71
  561.6 4.5 dynamic_update_slice.71
  575.7 4.5 dynamic_update_slice.71
  589.8 4.5 dynamic_update_slice.71
  594.7 41.4 %subtract_select_fusion.16 = bf16[960,16384]{1,0:T(8,128)(2,1)} fusion(f32[960,16384]{1,0:T(8,128)} %constant_dynamic-update-slice_fusion.3, f32[960,128]{0,1:T(8,128)S(1)} %get-tuple-element.576, bf16[128,16384]{1,0:T(8,128)(2,1)} %all-gather.12.cloned.1.call-done, pred[16384]{0:T(1024)(128)(4,1)S(1)} %iota_compare_fusion.35), kind=kOutput, calls=%fused_computation.144 | convolution fusion | flops 24190648320 | bytes 99074048 | tf_op jit(solution)/shard_map/dot_general | solution.py:98
  636.8 21.8 %copy.170 = bf16[120,8,8,2048]{3,2,0,1:T(8,128)(2,1)} copy(bf16[120,8,8,2048]{3,2,1,0:T(8,128)(2,1)} %bitcast.318) | data formatting | bytes 62914560 | tf_op jit(solution)/shard_map/all_to_all | solution.py:107
  658.6 688.0 %all_to_all.19 = bf16[960,8,2048]{2,0,1:T(8,128)(2,1)} all-to-all(bf16[960,8,2048]{2,0,1:T(8,128)(2,1)} %bitcast.320), channel_id=1, replica_groups=mesh['tok'=4,'tp'=8] {'tp'}, dimensions={1} | all-to-all | bytes 62914560 | tf_op jit(solution)/shard_map/all_to_all | solution.py:107
  1346.6 18.8 %convert_multiply_fusion = f32[4096,2048]{1,0:T(8,128)} fusion(bf16[4096,2048]{1,0:T(8,128)(2,1)} %reduce-scatter.4.cloned.1.call-done), kind=kLoop, calls=%fused_computation.147 | loop fusion | flops 16777216 | bytes 50331648 | tf_op jit(solution)/shard_map/div | solution.py:83
  1365.4 21.3 %copy.208 = bf16[7680,2048]{1,0:T(8,128)(2,1)} copy(bf16[7680,2048]{1,0:T(8,128)(2,1)} %bitcast.319) | data formatting | bytes 62914560
  (1126 shorter events, 312.9 us)
Async XLA Ops:
  7.2 60.1 %all-gather.14.cloned.1.call-start = ((), (), s32[]{:S(2)}) async-start(), calls=%async_computation.5 | async-start | bytes 1081344 | tf_op jit(solution)/shard_map/all_gather | solution.py:17
  8.7 285.7 %all-gather.16.cloned.1.call-start = ((), (), s32[]{:S(2)}) async-start(), calls=%async_computation.6 | async-start | bytes 1081344 | tf_op jit(solution)/shard_map/all_gather | solution.py:17
  9.4 286.3 %all-gather.10.cloned.1.call-start = ((), (), s32[]{:S(2)}) async-start(), calls=%async_computation.3 | async-start | bytes 4325376 | tf_op jit(solution)/shard_map/all_gather | solution.py:100
  11.2 328.9 %all-gather.8.cloned.1.call-start = ((), (), s32[]{:S(2)}) async-start(), calls=%async_computation.2 | async-start | bytes 9437184 | tf_op jit(solution)/shard_map/all_gather | solution.py:74
  34.7 560.0 %all-gather.12.cloned.1.call-start = ((), (), s32[]{:S(2)}) async-start(), calls=%async_computation.4 | async-start | bytes 4325376 | tf_op jit(solution)/shard_map/all_gather | solution.py:100
  35.3 1311.3 %reduce-scatter.4.cloned.1.call-start = ((), (), s32[]{:S(2)}) async-start(), calls=%async_computation.7 | async-start | bytes 83886080
  295.7 44.4 %copy-start = (bf16[256,2048]{1,0:T(8,128)(2,1)S(1)}, bf16[256,2048]{1,0:T(8,128)(2,1)}, u32[]{:S(2)}) copy-start(bf16[256,2048]{1,0:T(8,128)(2,1)} %fusion.64) | copy-start | bytes 3145732
Sparse Core Ops, SparseCore 0:
  11.0 56.2 all-gather.13
  70.2 52.8 all-gather.15
  126.1 62.1 all-gather.9
  190.9 121.4 all-gather.7
  315.8 62.4 all-gather.11
  380.7 444.5 reduce-scatter.3
